TPU v7x, 32 devices: a whole 2x2x4 slice. The times are simulated.
32 devices in a mesh: tm: 8 (over y, x, core), chan: 4 (over z).
Axes of the slice: x: 2, y: 2, z: 4, core: 2. Of those that a mesh axis runs over, the one named last changes fastest.
Arguments:
- volts: bfloat16 [4, 16, 12288, 256], P(None, 'chan', 'tm'), may hold values from -6 to 6
- delay_peak: int32 [128, 128], P('tm', 'chan'), may hold values from 0 to 32767
- rate_peak: int32 [128, 128], P('tm', 'chan'), may hold values from 0 to 15
- station_order: int32 [128], replicated, may hold values from 0 to 127, each once
- ref_station: int32 [1], replicated, may hold values from 0 to 63
Outputs:
- fringe: float32 [128, 128, 2, 8], P('tm', 'chan')
- normal: float32 [128, 2, 256], P('tm', None, 'chan')
- rhs: float32 [128, 2], P('tm')
Inputs may be any that keep to these rules, and one draw needn't show every extreme that they name: `station_order`: each input appears once.
All inputs are finite; a program needn't handle non-finite values.
Results may differ from a plain program's by a relative error of at most 0.0003.
Values sent between devices are 32-bit elements; how exact they have to be, the bound alone decides.
A program may use at most 64 MiB of HBM per device.

v0:
```python
import math

import jax
import jax.numpy as jnp
from jax import lax
from jax.sharding import PartitionSpec as P

BAND = 16384
PERIODS_ALL = 8
WD = 4
WR = 2


def fringe_window(vis_re, vis_im, dpeak, rpeak, chans_total, periods):
    chan_local = vis_re.shape[3]
    dgrid = 2 * BAND
    rgrid = 2 * PERIODS_ALL
    dstep = BAND // chans_total
    rstep = PERIODS_ALL // periods
    chan_idx = jnp.arange(chan_local, dtype=jnp.int32)
    period_idx = jnp.arange(periods, dtype=jnp.int32)
    delays = dpeak[:, :, None] + (jnp.arange(WD, dtype=jnp.int32) - WD // 2) * dstep
    rates = rpeak[:, :, None] + (jnp.arange(WR, dtype=jnp.int32) - WR // 2) * rstep
    dphase = jnp.mod(delays[..., None] * chan_idx, dgrid).astype(jnp.float32) * (
        2.0 * math.pi / dgrid
    )
    rphase = jnp.mod(rates[..., None] * period_idx, rgrid).astype(jnp.float32) * (
        2.0 * math.pi / rgrid
    )
    angle = rphase[:, :, :, None, :, None] + dphase[:, :, None, :, None, :]
    cosine = jnp.cos(angle)
    sine = jnp.sin(angle)
    vr = vis_re[:, :, None, None]
    vi = vis_im[:, :, None, None]
    fre = jnp.sum(vr * cosine + vi * sine, axis=(4, 5))
    fim = jnp.sum(vi * cosine - vr * sine, axis=(4, 5))
    return (fre, fim)


def baseline_weights(fre, fim):
    power = fre * fre + fim * fim
    udel = (2.0 * jnp.arange(WD, dtype=jnp.float32) + 1.0 - WD) / WD
    urat = (2.0 * jnp.arange(WR, dtype=jnp.float32) + 1.0 - WR) / WR
    udel = udel[None, :]
    urat = urat[:, None]
    m_dd = jnp.mean(power * udel * udel, axis=(2, 3))
    m_dr = jnp.mean(power * udel * urat, axis=(2, 3))
    m_rr = jnp.mean(power * urat * urat, axis=(2, 3))
    g_d = jnp.mean(power * udel, axis=(2, 3))
    g_r = jnp.mean(power * urat, axis=(2, 3))
    return jnp.stack([m_dd, m_dr, m_rr, g_d, g_r])


def normal_terms(weights, row_inputs, col_inputs, inputs):
    slots = jnp.arange(inputs, dtype=jnp.int32)
    incidence = (row_inputs[:, None, None] == slots).astype(jnp.float32) - (
        col_inputs[None, :, None] == slots
    ).astype(jnp.float32)
    flat = incidence.reshape(-1, inputs)

    def block(weight):
        scaled = (incidence * weight[:, :, None]).reshape(-1, inputs)
        return jnp.dot(scaled.T, flat, precision=lax.Precision.HIGHEST) / inputs

    n_dd = block(weights[0])
    n_dr = block(weights[1])
    n_rr = block(weights[2])
    normal = jnp.concatenate(
        [jnp.concatenate([n_dd, n_dr], 1), jnp.concatenate([n_dr, n_rr], 1)], 0
    )
    rhs_d = jnp.dot(weights[3].reshape(-1), flat, precision=lax.Precision.HIGHEST) / inputs
    rhs_r = jnp.dot(weights[4].reshape(-1), flat, precision=lax.Precision.HIGHEST) / inputs
    return (normal, jnp.concatenate([rhs_d, rhs_r]))


def full_gram(volts, inputs, scale):
    prod = jnp.einsum("acti,actj->iacj", volts, volts, preferred_element_type=jnp.float32)
    real = prod[:inputs, :, :, :inputs] + prod[inputs:, :, :, inputs:]
    imag = prod[:inputs, :, :, inputs:] - prod[inputs:, :, :, :inputs]
    return jnp.stack([real, imag], axis=3) * scale


def body(volts, delay_peak, rate_peak, station_order, ref_station):
    periods, chans, samples, width = volts.shape
    inputs = width // 2
    row_count = delay_peak.shape[0]
    col_count = delay_peak.shape[1]
    time_devs = lax.axis_size("tm")
    chan_devs = lax.axis_size("chan")
    chans_total = chans * chan_devs
    scale = float(samples * time_devs) ** (-0.5)
    spread = float(periods * chans_total) ** (-0.5)
    col_inputs = lax.dynamic_slice_in_dim(
        station_order, lax.axis_index("chan") * col_count, col_count
    )
    row_inputs = lax.axis_index("tm") * row_count + jnp.arange(row_count, dtype=jnp.int32)
    gram = full_gram(volts, inputs, scale)
    summed = lax.psum_scatter(
        gram.reshape(lax.axis_size("tm") * row_count, -1), "tm", scatter_dimension=0, tiled=True
    )
    vis = summed.reshape(row_count, periods, chans, 2, inputs)
    grouped = jnp.take(vis, station_order, axis=4)
    moved = lax.all_to_all(grouped, "chan", split_axis=4, concat_axis=2, tiled=True)
    vis_re = jnp.transpose(moved[:, :, :, 0], (0, 3, 1, 2))
    vis_im = jnp.transpose(moved[:, :, :, 1], (0, 3, 1, 2))
    fre, fim = fringe_window(vis_re, vis_im, delay_peak, rate_peak, chans_total, periods)
    auto = (row_inputs[:, None] == col_inputs[None, :])[:, :, None, None]
    fre = jnp.where(auto, 0.0, fre * spread)
    fim = jnp.where(auto, 0.0, fim * spread)
    fringe = jnp.stack([fre, fim], axis=2).reshape(row_count, col_count, 2, WR * WD)
    weights = baseline_weights(fre, fim)
    col_width = 2 * inputs // chan_devs
    normal_part, rhs_part = normal_terms(weights, row_inputs, col_inputs, inputs)
    arranged = jnp.transpose(normal_part.reshape(2, inputs, 2 * inputs), (1, 0, 2))
    arranged = arranged.reshape(time_devs, row_count, 2, chan_devs, col_width)
    arranged = jnp.transpose(arranged, (0, 3, 1, 2, 4)).reshape(
        time_devs * chan_devs * row_count, 2, col_width
    )
    normal_rows = lax.psum_scatter(arranged, ("tm", "chan"), scatter_dimension=0, tiled=True)
    rhs_all = lax.psum(jnp.transpose(rhs_part.reshape(2, inputs), (1, 0)), ("tm", "chan"))
    rhs_rows = lax.dynamic_slice_in_dim(rhs_all, lax.axis_index("tm") * row_count, row_count, 0)
    columns = lax.axis_index("chan") * col_width + jnp.arange(col_width, dtype=jnp.int32)
    params = jnp.arange(2, dtype=jnp.int32)[None, :] * inputs + row_inputs[:, None]
    row_ref = row_inputs // 2 == ref_station[0]
    col_ref = columns % inputs // 2 == ref_station[0]
    ident = (params[:, :, None] == columns[None, None, :]).astype(jnp.float32)
    normal_rows = jnp.where(row_ref[:, None, None] | col_ref[None, None, :], ident, normal_rows)
    rhs_rows = jnp.where(row_ref[:, None], 0.0, rhs_rows)
    return (fringe, normal_rows, rhs_rows)


def solution(mesh):
    in_specs = (P(None, "chan", "tm", None), P("tm", "chan"), P("tm", "chan"), P(), P())
    out_specs = (P("tm", "chan", None, None), P("tm", None, "chan"), P("tm", None))
    return jax.shard_map(body, mesh=mesh, in_specs=in_specs, out_specs=out_specs, check_vma=False)
```

profile of v0, /device:TPU:0, one launch (start us, length us, event | category | flops | bytes accessed | tf_op | source)
XLA Modules:
  0.0 298.8 jit_solution(5013165204191400454)
XLA Ops:
  7.2 0.0 reduce-scatter.7.cloned.1.call-start
  7.2 11.0 %convolution_bitcast_fusion = f32[256,4,4,256]{0,3,2,1:T(8,128)S(1)} fusion(bf16[4,4,1536,256]{3,2,1,0:T(8,128)(2,1)} %param.5), kind=kOutput, calls=%fused_computation.11 | convolution fusion | flops 3221225472 | bytes 16777216 | tf_op jit(solution)/shard_map/acti,actj->iacj/dot_general | solution.py:77
  18.2 0.2 fusion.19
  18.5 0.3 maximum_multiply_fusion
  18.7 0.2 copy.39
  19.0 1.9 copy.56
  21.5 0.1 dynamic_slice.6
  21.7 0.1 broadcast_add_fusion.2
  21.8 0.1 broadcast_compare_fusion
  21.9 0.1 broadcast_or_fusion
  21.9 0.1 fusion.43
  22.0 0.1 fusion.42
  22.1 0.1 broadcast_add_fusion.1
  22.2 0.1 broadcast_add_fusion
  22.2 0.1 fusion.41
  22.3 42.6 %reduce-scatter.7.cloned.1.call-done = f32[16,4096]{1,0:T(8,128)} async-done(((f32[128,4096]{1,0:T(8,128)}), f32[16,4096]{1,0:T(8,128)}) %reduce-scatter.7.cloned.1.call-update) | async-done | bytes 262160
  64.9 1.5 copy.57
  66.5 2.7 copy.41
  69.2 4.9 %gather_fusion = f32[128,16,4,4,2]{1,3,4,2,0:T(4,128)} fusion(f32[16,4,4,2,128]{0,2,4,3,1:T(4,128)} %copy.41, s32[1024]{0:T(1024)S(1)} %pad_clamp_fusion), kind=kCustom, calls=%fused_computation | custom fusion | bytes 524800 | tf_op jit(solution)/shard_map/jit(_take)/gather | solution.py:102
  74.1 2.1 fusion.47
  76.2 2.3 reshape.374
  78.5 4.6 %all-to-all-start = ((f32[4,1,16384]{2,1,0:T(1,128)}), f32[4,1,16384]{2,1,0:T(1,128)S(1)}, u32[]{:S(2)}, u32[]{:S(2)}) async-start(f32[4,1,16384]{2,1,0:T(1,128)} %reshape.374), calls=%async_computation | async-start | bytes 524288 | tf_op jit(solution)/shard_map/all_to_all | solution.py:103
  83.1 1.0 fusion.22
  84.2 7.9 %all-to-all-done = f32[4,1,16384]{2,1,0:T(1,128)S(1)} async-done(((f32[4,1,16384]{2,1,0:T(1,128)}), f32[4,1,16384]{2,1,0:T(1,128)S(1)}, u32[]{:S(2)}, u32[]{:S(2)}) %all-to-all-start) | async-done | bytes 262176 | tf_op jit(solution)/shard_map/all_to_all | solution.py:103
  92.0 0.5 broadcast.559
  92.5 1.4 reduce
  93.9 1.5 reshape.375
  95.4 1.0 copy.42
  96.4 0.1 slice_bitcast_fusion.1
  96.5 0.2 copy.43
  96.7 0.2 copy.44
  96.9 0.6 copy-done
  97.4 16.5 %fusion.5 = (f32[16,32,2,4]{1,3,2,0:T(4,128)S(1)}, f32[16,32,2,4]{1,3,2,0:T(4,128)S(1)}) fusion(f32[16,32,4,16]{1,3,2,0:T(8,128)S(1)} %copy.44, f32[16,32,4,16]{1,3,2,0:T(8,128)S(1)} %copy-done, f32[16,32,2,4]{1,3,2,0:T(4,128)S(1)} %fusion.41, f32[16,32,4,16]{1,3,2,0:T(8,128)S(1)} %copy.43), kind=kLoop, calls=%fused_computation.8 | loop fusion | flops 2351104 | bytes 442368 | tf_op jit(solution)/shard_map/reduce_sum | solution.py:35
  113.9 0.2 multiply_reduce_fusion.4
  114.2 0.3 fusion.12
  114.5 0.3 fusion.11
  114.8 37.9 %psum.7 = f32[128,2]{0,1:T(2,128)S(1)} all-reduce(f32[128,2]{0,1:T(2,128)S(1)} %maximum_bitcast_fusion), channel_id=1, replica_groups=mesh['tm'=8,'chan'=4] {'tm','chan'}, use_global_device_ids=true, to_apply=%region_9.10 | all-reduce | flops 256 | bytes 2048 | tf_op jit(solution)/shard_map/psum | solution.py:120
  152.7 0.7 fusion.9
  153.4 0.7 fusion.8
  154.1 0.7 fusion.10
  154.8 0.1 copy.55
  154.9 0.2 reshape.353
  155.2 0.8 copy.48
  156.0 0.7 pad_maximum_fusion
  156.7 0.6 dynamic-slice_select_fusion
  157.3 133.2 %reduce-scatter.5.cloned.1.call-done = f32[16,2,64]{2,0,1:T(8,128)} async-done(((f32[512,2,64]{2,0,1:T(8,128)}), f32[16,2,64]{2,0,1:T(8,128)}) %reduce-scatter.5.cloned.1.call-update) | async-done | bytes 8208 | tf_op jit(solution)/shard_map/reduce_scatter | solution.py:119
  290.5 0.8 convert_select_fusion
  291.3 0.6 copy.49
  (29 shorter events, 0.3 us)
Async XLA Ops:
  7.2 57.8 %reduce-scatter.7.cloned.1.call-start = ((), (), s32[]{:S(2)}) async-start(), calls=%async_computation.4 | async-start | bytes 2359296
  19.0 2.6 copy-start.3
  19.0 3.1 %copy-start.1 = (s32[16,32]{1,0:T(8,128)S(1)}, s32[16,32]{1,0:T(8,128)}, u32[]{:S(2)}) copy-start(s32[16,32]{1,0:T(8,128)} %param.7) | copy-start | bytes 6148
  19.0 3.2 %copy-start.2 = (s32[16,32]{1,0:T(8,128)S(1)}, s32[16,32]{1,0:T(8,128)}, u32[]{:S(2)}) copy-start(s32[16,32]{1,0:T(8,128)} %param.6) | copy-start | bytes 6148
  78.5 13.5 %all-to-all-start = ((f32[4,1,16384]{2,1,0:T(1,128)}), f32[4,1,16384]{2,1,0:T(1,128)S(1)}, u32[]{:S(2)}, u32[]{:S(2)}) async-start(f32[4,1,16384]{2,1,0:T(1,128)} %reshape.374), calls=%async_computation | async-start | bytes 524288 | tf_op jit(solution)/shard_map/all_to_all | solution.py:103
  83.1 207.4 %reduce-scatter.5.cloned.1.call-start = ((), (), s32[]{:S(2)}) async-start(), calls=%async_computation.3 | async-start | bytes 540672 | tf_op jit(solution)/shard_map/reduce_scatter | solution.py:119
  96.4 1.0 copy-start
Sparse Core Ops, SparseCore 0:
  21.0 43.8 reduce-scatter.6
  156.1 134.3 reduce-scatter.4
where the time goes:
time: 299 us
  waiting for transfers between devices  184 us (62%)
  blocking collectives  37.9 us (13%)
  other arithmetic  24.6 us (8%)
  local copies, waits for them, and re-layouts  19.4 us (6%)
  between operations  15 us (5%)
  matrix products  13.6 us (5%)
  starting transfers between devices  4.65 us (2%)
    reduce_scatter x1, waiting for transfers between devices, body(): lax.psum_scatter(arranged, ('tm', 'chan'), scatter_dimension=0, tiled=True)  133 us
    unnamed x3, waiting for transfers between devices  42.6 us
    psum x1, blocking collectives, body(): lax.psum(jnp.transpose(rhs_part.reshape(2, inputs), (1, 0)), ('tm', 'chan'))  37.9 us
    reduce_sum x1, other arithmetic, fringe_window(): fre = jnp.sum(vr * cosine + vi * sine, axis=(4, 5))  16.5 us
    dot_general x1, matrix products, full_gram(): jnp.einsum('acti,actj->iacj', volts, volts, preferred_element_type=jnp.fl...  11 us
    unnamed x13, local copies, waits for them, and re-layouts  8.36 us
    all_to_all x1, waiting for transfers between devices, body(): lax.all_to_all(grouped, 'chan', split_axis=4, concat_axis=2, tiled=True)  7.86 us
  transfers between devices with their start and end apart: 3, of which 3 were waited for; matrix products, arithmetic and copies ran while one was open for 1% of the time, Pallas kernels for 0%

commit v1 on v0

--- a/solution.py
+++ b/solution.py
@@ -1,8 +1,11 @@
+import functools
 import math
 
 import jax
 import jax.numpy as jnp
 from jax import lax
+from jax.experimental import pallas as pl
+from jax.experimental.pallas import tpu as pltpu
 from jax.sharding import PartitionSpec as P
 
 BAND = 16384
@@ -129,7 +132,386 @@
     return (fringe, normal_rows, rhs_rows)
 
 
+TM = 8
+MESH = pl.DeviceIdType.MESH
+TURN = 2 * BAND
+
+
+def unit(steps):
+    quarter = TURN // 4
+    quad = lax.shift_right_logical(steps + quarter // 2, quarter.bit_length() - 1)
+    x = (steps - quad * quarter).astype(jnp.float32) * (2.0 * math.pi / TURN)
+    y = x * x
+    s = x * (1.0 + y * (-1.0 / 6 + y * (1.0 / 120 + y * (-1.0 / 5040 + y * (1.0 / 362880)))))
+    c = 1.0 + y * (-0.5 + y * (1.0 / 24 + y * (-1.0 / 720 + y * (1.0 / 40320 + y * (-1.0 / 3628800)))))
+    odd = (quad & 1) == 1
+    cosine = jnp.where(odd, s, c)
+    sine = jnp.where(odd, c, s)
+    cosine = jnp.where(((quad + 1) & 2) == 2, -cosine, cosine)
+    sine = jnp.where((quad & 2) == 2, -sine, sine)
+    return cosine, sine
+
+
+def cmul(a, b):
+    return a[0] * b[0] - a[1] * b[1], a[0] * b[1] + a[1] * b[0]
+
+
+def cadd(a, b):
+    return b if a is None else (a[0] + b[0], a[1] + b[1])
+
+
+def cconst(a, turns):
+    turns = turns % 1.0
+    if turns == 0.0:
+        return a
+    if turns == 0.25:
+        return a[1], -a[0]
+    if turns == 0.5:
+        return -a[0], -a[1]
+    if turns == 0.75:
+        return -a[1], a[0]
+    c, s = math.cos(2 * math.pi * turns), math.sin(2 * math.pi * turns)
+    return a[0] * c + a[1] * s, a[1] * c - a[0] * s
+
+
+def fused(
+    nchan, volts, dpk, rpk, order, ref, fringe_out, normal_out, rhs_out,
+    xbuf, vre, vim, pkl, pka, pkb, part, sbuf, rb1, rb2, zs, rz, wz, nat, rx,
+    vsem, asend, arecv, bsend, brecv, s1, r1, s2, r2, s3, r3, s4, r4, s5, r5,
+):
+    i, j = lax.axis_index("tm"), lax.axis_index("chan")
+    periods, chans, samples, width = volts.shape
+    inputs = width // 2
+    rows, cols = dpk.shape
+    chans_total = chans * nchan
+    core, cx, cy = i % 2, (i // 2) % 2, i // 4
+    sibling = i + 1 - 2 * core
+    scale = float(samples * TM) ** (-0.5) * float(periods * chans_total) ** (-0.5)
+
+    def chip(r, c):
+        return ((((cy + r // 2) % 2) * 2) + (cx + r % 2) % 2) * 2 + c
+
+    def load(n):
+        return pltpu.make_async_copy(volts.at[n // chans, n % chans], xbuf.at[n], vsem.at[n])
+
+    def remote(src, dst, ssem, rsem, to_i, to_j):
+        return pltpu.make_async_remote_copy(
+            src_ref=src, dst_ref=dst, send_sem=ssem, recv_sem=rsem,
+            device_id=(to_i, to_j), device_id_type=MESH,
+        )
+
+    @pl.loop(0, periods * chans)
+    def _(n):
+        load(n).start()
+
+    pkl[...] = jnp.zeros_like(pkl)
+    pkl[:, 0:cols] = dpk[...]
+    pkl[:, cols : 2 * cols] = rpk[...]
+
+    barrier = pltpu.get_barrier_semaphore()
+    for d in range(1, TM):
+        pl.semaphore_signal(barrier, inc=1, device_id=((i + d) % TM, j), device_id_type=MESH)
+    for d in range(1, nchan):
+        pl.semaphore_signal(barrier, inc=1, device_id=(i, (j + d) % nchan), device_id_type=MESH)
+    pl.semaphore_wait(barrier, TM - 1 + nchan - 1)
+
+    acopies = [
+        remote(pkl, pka.at[d - 1], asend.at[d - 1], arecv.at[d - 1], i, (j + d) % nchan)
+        for d in range(1, nchan)
+    ]
+    for copy in acopies:
+        copy.start()
+
+    def gram(n):
+        load(n).wait()
+        x = xbuf[n]
+        g = lax.dot_general(x, x, (((0,), (0,)), ((), ())), preferred_element_type=jnp.float32)
+        vre[n] = g[:inputs, :inputs] + g[inputs:, inputs:]
+        vim[n] = g[:inputs, inputs:] - g[inputs:, :inputs]
+
+    @pl.loop(0, 4)
+    def _(n):
+        gram(n)
+
+    hot = (
+        lax.broadcasted_iota(jnp.int32, (inputs, inputs), 0)
+        == jnp.broadcast_to(order[...], (inputs, inputs))
+    ).astype(jnp.float32)
+    hot_t = hot.T
+
+    for copy in acopies:
+        copy.wait()
+    blocks = [pkl[...]] + [pka[d] for d in range(nchan - 1)]
+    ordered = []
+    for g in range(nchan):
+        pick = blocks[0]
+        for d in range(1, nchan):
+            pick = jnp.where((j + nchan - d) % nchan == g, blocks[d], pick)
+        ordered.append(pick)
+    dall = jnp.concatenate([b[:, 0:cols] for b in ordered], axis=1)
+    rall = jnp.concatenate([b[:, cols : 2 * cols] for b in ordered], axis=1)
+    digits = jnp.concatenate(
+        [
+            lax.shift_right_logical(dall, 8).astype(jnp.float32),
+            (dall & 255).astype(jnp.float32),
+            rall.astype(jnp.float32),
+        ],
+        axis=0,
+    )
+    moved = jnp.dot(
+        digits.astype(jnp.bfloat16), hot_t.astype(jnp.bfloat16), preferred_element_type=jnp.float32
+    )
+    pkb[i, 0] = (moved[0:rows] * 256.0 + moved[rows : 2 * rows]).astype(jnp.int32)
+    pkb[i, 1] = moved[2 * rows : 3 * rows].astype(jnp.int32)
+    bcopies = [
+        remote(pkb.at[i], pkb.at[i], bsend.at[d - 1], brecv.at[d - 1], (i + d) % TM, j)
+        for d in range(1, TM)
+    ]
+    for copy in bcopies:
+        copy.start()
+
+    @pl.loop(4, periods * chans)
+    def _(n):
+        gram(n)
+
+    for copy in bcopies:
+        copy.wait()
+
+    def by_chan(values):
+        pick = jnp.float32(values[0])
+        for g in range(1, nchan):
+            pick = jnp.where(j == g, jnp.float32(values[g]), pick)
+        return pick
+
+    dturn = (BAND // chans_total) / TURN
+    rturn = (PERIODS_ALL // periods) / (2 * PERIODS_ALL)
+    shifts = []
+    for wd in range(WD):
+        angles = [2 * math.pi * (wd - WD // 2) * g * chans * dturn for g in range(nchan)]
+        shifts.append(
+            (by_chan([math.cos(t) for t in angles]), by_chan([-math.sin(t) for t in angles]))
+        )
+
+    def window(ip, h):
+        at = pl.ds(pl.multiple_of(ip * rows + h * 8, 8), 8)
+        dl = pkb[ip, 0, h * 8 : h * 8 + 8, :]
+        rl = pkb[ip, 1, h * 8 : h * 8 + 8, :]
+        c, s = unit(dl)
+        z1 = (c, -s)
+        c, s = unit((dl * (j * chans)) & (TURN - 1))
+        ed = (c, -s)
+        c, s = unit(rl * (BAND // PERIODS_ALL))
+        er = [None, (c, -s)]
+        for a in range(2, periods):
+            er.append(cmul(er[-1], er[1]))
+        acc = [None] * (WR * WD)
+        for l in range(chans):
+            us = [None] * WR
+            for a in range(periods):
+                v = (vre[a * chans + l, at, :], vim[a * chans + l, at, :])
+                if a:
+                    v = cmul(v, er[a])
+                for wr in range(WR):
+                    us[wr] = cadd(us[wr], cconst(v, (wr - WR // 2) * a * rturn))
+            if l:
+                ed = cmul(ed, z1)
+            for wr in range(WR):
+                u = cmul(us[wr], ed)
+                for wd in range(WD):
+                    term = cconst(u, (wd - WD // 2) * l * dturn)
+                    acc[wr * WD + wd] = cadd(acc[wr * WD + wd], term)
+        out = []
+        for w in range(WR * WD):
+            wd = w % WD
+            out.append(acc[w] if wd == WD // 2 else cmul(acc[w], shifts[wd]))
+        return [o[0] for o in out] + [o[1] for o in out]
+
+    @pl.loop(0, 8)
+    def _(u):
+        r = 3 - u % 4
+        first = u < 4
+        side = jnp.where(first, 1 - core, core)
+        ip = chip(r, side)
+        for h in range(rows // 8):
+            values = window(ip, h)
+            for v, value in enumerate(values):
+                part[u, v, h * 8 : h * 8 + 8, :] = value
+
+        @pl.when(first)
+        def _():
+            remote(part.at[u], rb1.at[r], s1.at[r], r1.at[r], sibling, j).start()
+
+        @pl.when(u >= 4)
+        def _():
+            remote(part.at[3 - r], rb1.at[r], s1.at[r], r1.at[r], sibling, j).wait()
+            sbuf[r] = part[u] + rb1[r]
+
+            @pl.when(r > 0)
+            def _():
+                remote(sbuf.at[r], rb2.at[r - 1], s2.at[r - 1], r2.at[r - 1], chip(r, core), j).start()
+
+    bins = WR * WD
+    row = lax.broadcasted_iota(jnp.int32, (bins * rows, inputs), 0)
+    col = lax.broadcasted_iota(jnp.int32, (bins * rows, inputs), 1)
+    w_row, kind = row // rows, col // rows
+    ud = (2 * (w_row % WD) + 1 - WD).astype(jnp.float32) / WD
+    ur = (2 * (w_row // WD) + 1 - WR).astype(jnp.float32) / WR
+    coef = jnp.where(kind == 0, ud * ud, 0.0)
+    coef = jnp.where(kind == 1, ud * ur, coef)
+    coef = jnp.where(kind == 2, ur * ur, coef)
+    coef = jnp.where(kind == 3, ud, coef)
+    coef = jnp.where(kind == 4, ur, coef)
+    coef = jnp.where(row % rows == col % rows, coef, 0.0) * (1.0 / bins)
+
+    for r in (1, 2, 3):
+        remote(sbuf.at[r], rb2.at[r - 1], s2.at[r - 1], r2.at[r - 1], chip(r, core), j).wait()
+    total = (sbuf[0] + rb2[0]) + (rb2[1] + rb2[2])
+    shape3 = (2 * bins, rows, inputs)
+    auto = lax.broadcasted_iota(jnp.int32, shape3, 2) == (
+        lax.broadcasted_iota(jnp.int32, shape3, 1) + i * rows
+    )
+    total = jnp.where(auto, 0.0, total * scale).reshape(2 * bins * rows, inputs)
+    zs[...] = lax.dot_general(
+        hot_t, total, (((1,), (1,)), ((), ())),
+        precision=lax.Precision.HIGHEST, preferred_element_type=jnp.float32,
+    )
+
+    def group(g):
+        return pl.ds(pl.multiple_of(g * cols, cols), cols)
+
+    copies = []
+    for d in range(1, nchan):
+        to = (j + d) % nchan
+        copies.append(remote(zs.at[group(to)], rz.at[d - 1], s3.at[d - 1], r3.at[d - 1], i, to))
+        copies[-1].start()
+    mine = zs[group(j), :]
+    for d, copy in enumerate(copies):
+        copy.wait()
+        mine = mine + rz[d]
+    fringe_out[...] = mine
+    fre, fim = mine[:, : bins * rows], mine[:, bins * rows :]
+    power = fre * fre + fim * fim
+    wz[group(j), :] = jnp.dot(
+        power, coef, precision=lax.Precision.HIGHEST, preferred_element_type=jnp.float32
+    )
+    copies = []
+    for d in range(1, nchan):
+        to = (j + d) % nchan
+        copies.append(remote(wz.at[group(j)], wz.at[group(j)], s4.at[d - 1], r4.at[d - 1], i, to))
+        copies[-1].start()
+    for copy in copies:
+        copy.wait()
+    natural = jnp.dot(
+        hot, wz[...], precision=lax.Precision.HIGHEST, preferred_element_type=jnp.float32
+    )
+    nat[...] = natural
+
+    def rowsof(g):
+        return pl.ds(pl.multiple_of(g * rows, rows), rows)
+
+    copies = []
+    for d in range(1, TM):
+        to = (i + d) % TM
+        copies.append(remote(nat.at[rowsof(to)], rx.at[i], s5.at[d - 1], r5.at[d - 1], to, j))
+        copies[-1].start()
+    rx[i] = nat[rowsof(i), :]
+    straight = natural.T
+    for copy in copies:
+        copy.wait()
+    across = [
+        jnp.concatenate([rx[g, :, m * rows : (m + 1) * rows] for g in range(TM)], axis=1)
+        for m in range(5)
+    ]
+    straight = [straight[m * rows : (m + 1) * rows] for m in range(5)]
+    row_in = lax.broadcasted_iota(jnp.int32, (rows, inputs), 0) + i * rows
+    col_in = lax.broadcasted_iota(jnp.int32, (rows, inputs), 1)
+    diag = row_in == col_in
+    isref = (lax.shift_right_logical(row_in, 1) == ref[0]) | (
+        lax.shift_right_logical(col_in, 1) == ref[0]
+    )
+    blocks = []
+    for m in range(3):
+        both = straight[m] + across[m]
+        sums = jnp.sum(both, axis=1, keepdims=True)
+        blocks.append((jnp.where(diag, sums, 0.0) - both) * (1.0 / inputs))
+    t = j * 2 // nchan
+    per = nchan // 2
+    span = 2 * inputs // nchan
+    for s in range(2):
+        block = jnp.where(t == 0, blocks[s], blocks[s + 1])
+        ident = jnp.where(diag & (t == s), 1.0, 0.0)
+        block = jnp.where(isref, ident, block)
+        out = block[:, 0:span]
+        for q in range(1, per):
+            out = jnp.where(j % per == q, block[:, q * span : (q + 1) * span], out)
+        normal_out[:, s, :] = out
+    row_ref = lax.shift_right_logical(
+        lax.broadcasted_iota(jnp.int32, (rows, 1), 0) + i * rows, 1
+    ) == ref[0]
+    for s in range(2):
+        value = jnp.sum(straight[3 + s] - across[3 + s], axis=1, keepdims=True) * (1.0 / inputs)
+        rhs_out[:, s : s + 1] = jnp.where(row_ref, 0.0, value)
+
+
+def fused_body(nchan, volts, delay_peak, rate_peak, station_order, ref_station):
+    periods, chans, samples, width = volts.shape
+    inputs = width // 2
+    rows, cols = delay_peak.shape
+    bins = WR * WD
+    steps = periods * chans
+    f32 = jnp.float32
+    vmem = pl.BlockSpec(memory_space=pltpu.VMEM)
+    dma = pltpu.SemaphoreType.DMA
+    fringe, normal, rhs = pl.pallas_call(
+        functools.partial(fused, nchan),
+        out_shape=(
+            jax.ShapeDtypeStruct((cols, 2 * bins * rows), f32),
+            jax.ShapeDtypeStruct((rows, 2, 2 * inputs // nchan), f32),
+            jax.ShapeDtypeStruct((rows, 2), f32),
+        ),
+        in_specs=[
+            pl.BlockSpec(memory_space=pl.ANY), vmem, vmem, vmem,
+            pl.BlockSpec(memory_space=pltpu.SMEM),
+        ],
+        out_specs=(vmem, vmem, vmem),
+        scratch_shapes=[
+            pltpu.VMEM((steps, samples, width), volts.dtype),
+            pltpu.VMEM((steps, inputs, inputs), f32),
+            pltpu.VMEM((steps, inputs, inputs), f32),
+            pltpu.VMEM((rows, inputs), jnp.int32),
+            pltpu.VMEM((nchan - 1, rows, inputs), jnp.int32),
+            pltpu.VMEM((TM, 2, rows, inputs), jnp.int32),
+            pltpu.VMEM((TM, 2 * bins, rows, inputs), f32),
+            pltpu.VMEM((4, 2 * bins, rows, inputs), f32),
+            pltpu.VMEM((4, 2 * bins, rows, inputs), f32),
+            pltpu.VMEM((3, 2 * bins, rows, inputs), f32),
+            pltpu.VMEM((inputs, 2 * bins * rows), f32),
+            pltpu.VMEM((nchan - 1, cols, 2 * bins * rows), f32),
+            pltpu.VMEM((inputs, inputs), f32),
+            pltpu.VMEM((inputs, inputs), f32),
+            pltpu.VMEM((TM, rows, inputs), f32),
+            dma((steps,)),
+            dma((nchan - 1,)), dma((nchan - 1,)),
+            dma((TM - 1,)), dma((TM - 1,)),
+            dma((4,)), dma((4,)),
+            dma((3,)), dma((3,)),
+            dma((nchan - 1,)), dma((nchan - 1,)),
+            dma((nchan - 1,)), dma((nchan - 1,)),
+            dma((TM - 1,)), dma((TM - 1,)),
+        ],
+        compiler_params=pltpu.CompilerParams(
+            collective_id=0, has_side_effects=True, vmem_limit_bytes=48 * 1024 * 1024
+        ),
+        name="fringe_fit",
+    )(volts, delay_peak, rate_peak, station_order.reshape(1, inputs), ref_station)
+    fringe = jnp.transpose(fringe.reshape(cols, 2, bins, rows), (3, 0, 1, 2))
+    return fringe, normal, rhs
+
+
 def solution(mesh):
     in_specs = (P(None, "chan", "tm", None), P("tm", "chan"), P("tm", "chan"), P(), P())
     out_specs = (P("tm", "chan", None, None), P("tm", None, "chan"), P("tm", None))
-    return jax.shard_map(body, mesh=mesh, in_specs=in_specs, out_specs=out_specs, check_vma=False)
+    nchan = mesh.shape["chan"]
+    fits = mesh.shape["tm"] == TM and nchan == 4
+    whole = functools.partial(fused_body, nchan) if fits else body
+    return jax.shard_map(whole, mesh=mesh, in_specs=in_specs, out_specs=out_specs, check_vma=False)

time: 299 us -> 42.4 us (0.14)
  waiting for transfers between devices: 184 us -> 0 us
  blocking collectives: 37.9 us -> 0 us
  Pallas kernels: 0 us -> 36.8 us
  other arithmetic: 24.6 us -> 0 us
  local copies, waits for them, and re-layouts: 19.4 us -> 4.08 us
  between operations: 15 us -> 1.3 us
  matrix products: 13.6 us -> 0 us
  starting transfers between devices: 4.65 us -> 0 us
    reduce_scatter x1 -> x0, waiting for transfers between devices: 133 us -> none  [body(): lax.psum_scatter(arranged, ('tm', 'chan'), scatter_dimension=0, tiled=True)]
    unnamed x3 -> x0, waiting for transfers between devices: 42.6 us -> none
    psum x1 -> x0, blocking collectives: 37.9 us -> none  [body(): lax.psum(jnp.transpose(rhs_part.reshape(2, inputs), (1, 0)), ('tm', 'chan'))]
    pallas_call x0 -> x1, Pallas kernels: none -> 36.8 us  [fused_body(): pl.pallas_call(functools.partial(fused, nchan), out_shape=(jax.ShapeDtype...]
    reduce_sum x2 -> x0, other arithmetic: 16.7 us -> none  [the longest x1 16.5 us: fringe_window(): fre = jnp.sum(vr * cosine + vi * sine, axis=(4, 5))]
    dot_general x6 -> x0, matrix products: 13.6 us -> none  [the longest x1 11 us: full_gram(): jnp.einsum('acti,actj->iacj', volts, volts, preferred_element_type=jnp.fl...]
    all_to_all x1 -> x0, waiting for transfers between devices: 7.86 us -> none  [body(): lax.all_to_all(grouped, 'chan', split_axis=4, concat_axis=2, tiled=True)]
    gather x1 -> x0, local copies, waits for them, and re-layouts: 4.92 us -> none  [body(): grouped = jnp.take(vis, station_order, axis=4)]
  transfers between devices with their start and end apart: 3 -> 0, of which waited for: 3 -> 0; matrix products, arithmetic and copies ran while one was open for 1% -> 0% of each run, Pallas kernels for 0% -> 0%
where the time goes in v1:
time: 42.4 us; the launch traced here: 42.1 us
  Pallas kernels  36.8 us (87%)
  local copies, waits for them, and re-layouts  4.08 us (10%)
  between operations  1.3 us (3%)
    pallas_call x1, Pallas kernels, fused_body(): pl.pallas_call(functools.partial(fused, nchan), out_shape=(jax.ShapeDtype...  36.8 us
    unnamed x9, local copies, waits for them, and re-layouts  3.98 us

profile of v1, /device:TPU:0, one launch (start us, length us, event | category | flops | bytes accessed | tf_op | source)
XLA Modules:
  0.0 42.1 jit_solution(16964748899990812420)
XLA Ops:
  1.3 0.0 copy-start
  1.3 0.7 %copy-done = s32[16,32]{1,0:T(8,128)S(1)} copy-done((s32[16,32]{1,0:T(8,128)S(1)}, s32[16,32]{1,0:T(8,128)}, u32[]{:S(2)}) %copy-start) | copy-done | bytes 2072
  2.0 0.0 copy-start.1
  2.0 0.7 %copy-done.1 = s32[16,32]{1,0:T(8,128)S(1)} copy-done((s32[16,32]{1,0:T(8,128)S(1)}, s32[16,32]{1,0:T(8,128)}, u32[]{:S(2)}) %copy-start.1) | copy-done | bytes 2072
  2.7 0.0 copy-start.2
  2.7 0.7 %copy-done.2 = s32[128]{0:T(128)S(1)} copy-done((s32[128]{0:T(128)S(1)}, s32[128]{0:T(128)}, u32[]{:S(2)}) %copy-start.2) | copy-done | bytes 536
  3.3 36.8 %fringe_fit.1 = (f32[32,256]{1,0:T(8,128)S(1)}, f32[16,2,64]{2,1,0:T(2,128)S(1)}, f32[16,2]{1,0:T(8,128)S(1)}) custom-call(bf16[4,4,1536,256]{3,2,1,0:T(8,128)(2,1)} %volts.1, s32[16,32]{1,0:T(8,128)S(1)} %copy-done, s32[16,32]{1,0:T(8,128)S(1)} %copy-done.1, s32[1,128]{1,0:T(1,128)S(1)} %bitcast.4, s32[1]{0:T(128)S(6)} %copy.14.ref), custom_call_target="tpu_custom_call" | custom-call | tf_op jit(solution)/shard_map/fringe_fit/pallas_call | solution.py:465
  40.1 0.6 %copy.12 = f32[16,2]{0,1:T(2,128)} copy(f32[16,2]{1,0:T(8,128)S(1)} %get-tuple-element.14) | data formatting | bytes 256
  40.7 0.1 copy.10
  40.8 0.7 %copy.11 = f32[16,32,2,8]{1,3,2,0:T(8,128)} copy(f32[16,32,2,8]{1,0,3,2:T(8,128)S(1)} %bitcast.5) | data formatting | bytes 65536
  41.5 0.6 %copy.15 = f32[16,2,64]{2,1,0:T(2,128)} copy(f32[16,2,64]{2,1,0:T(2,128)S(1)} %get-tuple-element.19) | data formatting | bytes 16384
Async XLA Ops:
  1.3 0.7 %copy-start = (s32[16,32]{1,0:T(8,128)S(1)}, s32[16,32]{1,0:T(8,128)}, u32[]{:S(2)}) copy-start(s32[16,32]{1,0:T(8,128)} %dpk.1) | copy-start | bytes 6148
  2.0 0.7 %copy-start.1 = (s32[16,32]{1,0:T(8,128)S(1)}, s32[16,32]{1,0:T(8,128)}, u32[]{:S(2)}) copy-start(s32[16,32]{1,0:T(8,128)} %rpk.1) | copy-start | bytes 6148
  2.7 0.7 %copy-start.2 = (s32[128]{0:T(128)S(1)}, s32[128]{0:T(128)}, u32[]{:S(2)}) copy-start(s32[128]{0:T(128)} %param.8) | copy-start | bytes 1540

commit v2 on v1

--- a/solution.py
+++ b/solution.py
@@ -175,9 +175,9 @@
 
 
 def fused(
-    nchan, volts, dpk, rpk, order, ref, fringe_out, normal_out, rhs_out,
-    xbuf, vre, vim, pkl, pka, pkb, part, sbuf, rb1, rb2, zs, rz, wz, nat, rx,
-    vsem, asend, arecv, bsend, brecv, s1, r1, s2, r2, s3, r3, s4, r4, s5, r5,
+    nchan, volts, dpk, rpk, order_in, ref, fringe_out, normal_out, rhs_out,
+    xbuf, dbuf, rbuf, order, vis, rv, pkl, pka, pnat, sbuf, rb2, zs, rz, wz, nat, rx,
+    vsem, isem, bsend, brecv, s1, r1, s2, r2, s3, r3, s4, r4, s5, r5,
 ):
     i, j = lax.axis_index("tm"), lax.axis_index("chan")
     periods, chans, samples, width = volts.shape
@@ -204,32 +204,51 @@
     def _(n):
         load(n).start()
 
-    pkl[...] = jnp.zeros_like(pkl)
-    pkl[:, 0:cols] = dpk[...]
-    pkl[:, cols : 2 * cols] = rpk[...]
+    small = [
+        pltpu.make_async_copy(src, dst, isem.at[n])
+        for n, (src, dst) in enumerate([(dpk, dbuf), (rpk, rbuf), (order_in, order)])
+    ]
+    for copy in small:
+        copy.start()
 
     barrier = pltpu.get_barrier_semaphore()
-    for d in range(1, TM):
-        pl.semaphore_signal(barrier, inc=1, device_id=((i + d) % TM, j), device_id_type=MESH)
-    for d in range(1, nchan):
-        pl.semaphore_signal(barrier, inc=1, device_id=(i, (j + d) % nchan), device_id_type=MESH)
-    pl.semaphore_wait(barrier, TM - 1 + nchan - 1)
-
-    acopies = [
-        remote(pkl, pka.at[d - 1], asend.at[d - 1], arecv.at[d - 1], i, (j + d) % nchan)
-        for d in range(1, nchan)
-    ]
-    for copy in acopies:
-        copy.start()
+    mates = [(r, d) for r in range(4) for d in range(nchan) if r or d]
+    for r, d in mates:
+        pl.semaphore_signal(
+            barrier, inc=1, device_id=(chip(r, core), (j + d) % nchan), device_id_type=MESH
+        )
+    for r in range(4):
+        pl.semaphore_signal(barrier, inc=1, device_id=(chip(r, 1 - core), j), device_id_type=MESH)
+
+    for copy in small:
+        copy.wait()
+    half = rows // 2
+    for h in range(2):
+        at = slice(h * half, h * half + half)
+        pkl[:, 2 * h * cols : (2 * h + 1) * cols] = dbuf[at, :]
+        pkl[:, (2 * h + 1) * cols : (2 * h + 2) * cols] = rbuf[at, :]
+    home = cy * 2 + cx
+    pka[home, j] = pkl[...]
 
     def gram(n):
         load(n).wait()
         x = xbuf[n]
         g = lax.dot_general(x, x, (((0,), (0,)), ((), ())), preferred_element_type=jnp.float32)
-        vre[n] = g[:inputs, :inputs] + g[inputs:, inputs:]
-        vim[n] = g[:inputs, inputs:] - g[inputs:, :inputs]
-
-    @pl.loop(0, 4)
+        re = g[:inputs, :inputs] + g[inputs:, inputs:]
+        im = g[:inputs, inputs:] - g[inputs:, :inputs]
+        for c in range(2):
+            for p in range(4):
+                at = slice((2 * p + c) * rows, (2 * p + c + 1) * rows)
+                vis[c, n, 0, p * rows : (p + 1) * rows, :] = re[at]
+                vis[c, n, 1, p * rows : (p + 1) * rows, :] = im[at]
+
+    def swap(n):
+        return remote(vis.at[1 - core, n], rv.at[n], s1.at[n], r1.at[n], sibling, j)
+
+    steps = periods * chans
+    early = 6
+
+    @pl.loop(0, early)
     def _(n):
         gram(n)
 
@@ -239,17 +258,43 @@
     ).astype(jnp.float32)
     hot_t = hot.T
 
-    for copy in acopies:
+    pl.semaphore_wait(barrier, len(mates) + 4)
+    bcopies = [
+        remote(pkl, pka.at[home, j], bsend.at[e], brecv.at[e], chip(r, core), (j + d) % nchan)
+        for e, (r, d) in enumerate(mates)
+    ]
+    for copy in bcopies:
+        copy.start()
+
+    @pl.loop(0, early)
+    def _(n):
+        swap(n).start()
+
+    @pl.loop(early, steps)
+    def _(n):
+        gram(n)
+        swap(n).start()
+
+    for copy in bcopies:
         copy.wait()
-    blocks = [pkl[...]] + [pka[d] for d in range(nchan - 1)]
-    ordered = []
-    for g in range(nchan):
-        pick = blocks[0]
-        for d in range(1, nchan):
-            pick = jnp.where((j + nchan - d) % nchan == g, blocks[d], pick)
-        ordered.append(pick)
-    dall = jnp.concatenate([b[:, 0:cols] for b in ordered], axis=1)
-    rall = jnp.concatenate([b[:, cols : 2 * cols] for b in ordered], axis=1)
+
+    def gathered(k):
+        return jnp.concatenate(
+            [
+                jnp.concatenate(
+                    [
+                        pka[c, g][:, (2 * h + k) * cols : (2 * h + k + 1) * cols]
+                        for g in range(nchan)
+                    ],
+                    axis=1,
+                )
+                for c in range(4)
+                for h in range(2)
+            ],
+            axis=0,
+        )
+
+    dall, rall = gathered(0), gathered(1)
     digits = jnp.concatenate(
         [
             lax.shift_right_logical(dall, 8).astype(jnp.float32),
@@ -261,21 +306,13 @@
     moved = jnp.dot(
         digits.astype(jnp.bfloat16), hot_t.astype(jnp.bfloat16), preferred_element_type=jnp.float32
     )
-    pkb[i, 0] = (moved[0:rows] * 256.0 + moved[rows : 2 * rows]).astype(jnp.int32)
-    pkb[i, 1] = moved[2 * rows : 3 * rows].astype(jnp.int32)
-    bcopies = [
-        remote(pkb.at[i], pkb.at[i], bsend.at[d - 1], brecv.at[d - 1], (i + d) % TM, j)
-        for d in range(1, TM)
-    ]
-    for copy in bcopies:
-        copy.start()
-
-    @pl.loop(4, periods * chans)
+    own = 4 * rows
+    pnat[0] = (moved[0:own] * 256.0 + moved[own : 2 * own]).astype(jnp.int32)
+    pnat[1] = moved[2 * own : 3 * own].astype(jnp.int32)
+
+    @pl.loop(0, steps)
     def _(n):
-        gram(n)
-
-    for copy in bcopies:
-        copy.wait()
+        swap(n).wait()
 
     def by_chan(values):
         pick = jnp.float32(values[0])
@@ -292,10 +329,10 @@
             (by_chan([math.cos(t) for t in angles]), by_chan([-math.sin(t) for t in angles]))
         )
 
-    def window(ip, h):
-        at = pl.ds(pl.multiple_of(ip * rows + h * 8, 8), 8)
-        dl = pkb[ip, 0, h * 8 : h * 8 + 8, :]
-        rl = pkb[ip, 1, h * 8 : h * 8 + 8, :]
+    def window(cc, h):
+        at = pl.ds(pl.multiple_of(cc * rows + h * 8, 8), 8)
+        dl = pnat[0, at, :]
+        rl = pnat[1, at, :]
         c, s = unit(dl)
         z1 = (c, -s)
         c, s = unit((dl * (j * chans)) & (TURN - 1))
@@ -308,7 +345,11 @@
         for l in range(chans):
             us = [None] * WR
             for a in range(periods):
-                v = (vre[a * chans + l, at, :], vim[a * chans + l, at, :])
+                n = a * chans + l
+                v = (
+                    vis[core, n, 0, at, :] + rv[n, 0, at, :],
+                    vis[core, n, 1, at, :] + rv[n, 1, at, :],
+                )
                 if a:
                     v = cmul(v, er[a])
                 for wr in range(WR):
@@ -326,29 +367,17 @@
             out.append(acc[w] if wd == WD // 2 else cmul(acc[w], shifts[wd]))
         return [o[0] for o in out] + [o[1] for o in out]
 
-    @pl.loop(0, 8)
+    @pl.loop(0, 4)
     def _(u):
-        r = 3 - u % 4
-        first = u < 4
-        side = jnp.where(first, 1 - core, core)
-        ip = chip(r, side)
+        r = 3 - u
         for h in range(rows // 8):
-            values = window(ip, h)
+            values = window(chip(r, core) // 2, h)
             for v, value in enumerate(values):
-                part[u, v, h * 8 : h * 8 + 8, :] = value
-
-        @pl.when(first)
+                sbuf[r, v, h * 8 : h * 8 + 8, :] = value
+
+        @pl.when(r > 0)
         def _():
-            remote(part.at[u], rb1.at[r], s1.at[r], r1.at[r], sibling, j).start()
-
-        @pl.when(u >= 4)
-        def _():
-            remote(part.at[3 - r], rb1.at[r], s1.at[r], r1.at[r], sibling, j).wait()
-            sbuf[r] = part[u] + rb1[r]
-
-            @pl.when(r > 0)
-            def _():
-                remote(sbuf.at[r], rb2.at[r - 1], s2.at[r - 1], r2.at[r - 1], chip(r, core), j).start()
+            remote(sbuf.at[r], rb2.at[r - 1], s2.at[r - 1], r2.at[r - 1], chip(r, core), j).start()
 
     bins = WR * WD
     row = lax.broadcasted_iota(jnp.int32, (bins * rows, inputs), 0)
@@ -388,7 +417,6 @@
     for d, copy in enumerate(copies):
         copy.wait()
         mine = mine + rz[d]
-    fringe_out[...] = mine
     fre, fim = mine[:, : bins * rows], mine[:, bins * rows :]
     power = fre * fre + fim * fim
     wz[group(j), :] = jnp.dot(
@@ -399,6 +427,8 @@
         to = (j + d) % nchan
         copies.append(remote(wz.at[group(j)], wz.at[group(j)], s4.at[d - 1], r4.at[d - 1], i, to))
         copies[-1].start()
+    turned = mine.T.reshape(2 * bins, rows, cols)
+    fringe_out[...] = jnp.swapaxes(turned, 0, 1)
     for copy in copies:
         copy.wait()
     natural = jnp.dot(
@@ -445,12 +475,18 @@
         for q in range(1, per):
             out = jnp.where(j % per == q, block[:, q * span : (q + 1) * span], out)
         normal_out[:, s, :] = out
-    row_ref = lax.shift_right_logical(
-        lax.broadcasted_iota(jnp.int32, (rows, 1), 0) + i * rows, 1
-    ) == ref[0]
+    lane = lax.broadcasted_iota(jnp.int32, (rows, inputs), 1)
+    right = jnp.zeros((rows, inputs), jnp.float32)
     for s in range(2):
         value = jnp.sum(straight[3 + s] - across[3 + s], axis=1, keepdims=True) * (1.0 / inputs)
-        rhs_out[:, s : s + 1] = jnp.where(row_ref, 0.0, value)
+        right = jnp.where(lane == s, value, right)
+    right = jnp.where(lax.shift_right_logical(row_in, 1) == ref[0], 0.0, right)
+    rhs_out[...] = right.T[0:2, :]
+
+
+def emit(*refs):
+    for src, dst in zip(refs[:3], refs[3:]):
+        dst[...] = src[...]
 
 
 def fused_body(nchan, volts, delay_peak, rate_peak, station_order, ref_station):
@@ -462,27 +498,27 @@
     f32 = jnp.float32
     vmem = pl.BlockSpec(memory_space=pltpu.VMEM)
     dma = pltpu.SemaphoreType.DMA
-    fringe, normal, rhs = pl.pallas_call(
+    out_shape = (
+        jax.ShapeDtypeStruct((rows, 2 * bins, cols), f32),
+        jax.ShapeDtypeStruct((rows, 2, 2 * inputs // nchan), f32),
+        jax.ShapeDtypeStruct((2, rows), f32),
+    )
+    hbm = pl.BlockSpec(memory_space=pltpu.HBM)
+    results = pl.pallas_call(
         functools.partial(fused, nchan),
-        out_shape=(
-            jax.ShapeDtypeStruct((cols, 2 * bins * rows), f32),
-            jax.ShapeDtypeStruct((rows, 2, 2 * inputs // nchan), f32),
-            jax.ShapeDtypeStruct((rows, 2), f32),
-        ),
-        in_specs=[
-            pl.BlockSpec(memory_space=pl.ANY), vmem, vmem, vmem,
-            pl.BlockSpec(memory_space=pltpu.SMEM),
-        ],
+        out_shape=out_shape,
+        in_specs=[hbm, hbm, hbm, hbm, pl.BlockSpec(memory_space=pltpu.SMEM)],
         out_specs=(vmem, vmem, vmem),
         scratch_shapes=[
             pltpu.VMEM((steps, samples, width), volts.dtype),
-            pltpu.VMEM((steps, inputs, inputs), f32),
-            pltpu.VMEM((steps, inputs, inputs), f32),
-            pltpu.VMEM((rows, inputs), jnp.int32),
-            pltpu.VMEM((nchan - 1, rows, inputs), jnp.int32),
-            pltpu.VMEM((TM, 2, rows, inputs), jnp.int32),
-            pltpu.VMEM((TM, 2 * bins, rows, inputs), f32),
-            pltpu.VMEM((4, 2 * bins, rows, inputs), f32),
+            pltpu.VMEM((rows, cols), jnp.int32),
+            pltpu.VMEM((rows, cols), jnp.int32),
+            pltpu.VMEM((1, inputs), jnp.int32),
+            pltpu.VMEM((2, steps, 2, 4 * rows, inputs), f32),
+            pltpu.VMEM((steps, 2, 4 * rows, inputs), f32),
+            pltpu.VMEM((rows // 2, 4 * cols), jnp.int32),
+            pltpu.VMEM((4, nchan, rows // 2, 4 * cols), jnp.int32),
+            pltpu.VMEM((2, 4 * rows, inputs), jnp.int32),
             pltpu.VMEM((4, 2 * bins, rows, inputs), f32),
             pltpu.VMEM((3, 2 * bins, rows, inputs), f32),
             pltpu.VMEM((inputs, 2 * bins * rows), f32),
@@ -490,10 +526,9 @@
             pltpu.VMEM((inputs, inputs), f32),
             pltpu.VMEM((inputs, inputs), f32),
             pltpu.VMEM((TM, rows, inputs), f32),
-            dma((steps,)),
-            dma((nchan - 1,)), dma((nchan - 1,)),
-            dma((TM - 1,)), dma((TM - 1,)),
-            dma((4,)), dma((4,)),
+            dma((steps,)), dma((3,)),
+            dma((4 * nchan - 1,)), dma((4 * nchan - 1,)),
+            dma((steps,)), dma((steps,)),
             dma((3,)), dma((3,)),
             dma((nchan - 1,)), dma((nchan - 1,)),
             dma((nchan - 1,)), dma((nchan - 1,)),
@@ -504,8 +539,12 @@
         ),
         name="fringe_fit",
     )(volts, delay_peak, rate_peak, station_order.reshape(1, inputs), ref_station)
-    fringe = jnp.transpose(fringe.reshape(cols, 2, bins, rows), (3, 0, 1, 2))
-    return fringe, normal, rhs
+    fringe, normal, rhs = pl.pallas_call(
+        emit, out_shape=out_shape, in_specs=[vmem] * 3, out_specs=(vmem,) * 3, name="emit",
+        compiler_params=pltpu.CompilerParams(vmem_limit_bytes=4 * 1024 * 1024),
+    )(*results)
+    fringe = jnp.transpose(fringe.reshape(rows, 2, bins, cols), (0, 3, 1, 2))
+    return fringe, normal, jnp.transpose(rhs)
 
 
 def solution(mesh):

time: 42.4 us -> 38.2 us (0.901)
  Pallas kernels: 36.8 us -> 34.6 us
  local copies, waits for them, and re-layouts: 4.08 us -> 2.04 us
    pallas_call x1 -> x2, Pallas kernels: 36.8 us -> 34.6 us  [the longest x1 33.9 us: fused_body(): pl.pallas_call(functools.partial(fused, nchan), out_shape=out_shape, in_s...]
    unnamed x9 -> x6, local copies, waits for them, and re-layouts: 3.98 us -> 2.04 us
where the time goes in v2:
time: 38.2 us; the launch traced here: 37.9 us
  Pallas kernels  34.6 us (91%)
  local copies, waits for them, and re-layouts  2.04 us (5%)
  between operations  1.3 us (3%)
    pallas_call x1, Pallas kernels, fused_body(): pl.pallas_call(functools.partial(fused, nchan), out_shape=out_shape, in_s...  33.9 us
    unnamed x6, local copies, waits for them, and re-layouts  2.04 us

profile of v2, /device:TPU:0, one launch (start us, length us, event | category | flops | bytes accessed | tf_op | source)
XLA Modules:
  0.0 37.9 jit_solution(17602519934872091090)
XLA Ops:
  1.3 0.0 copy-start
  1.3 0.7 %copy-done = s32[16,32]{1,0:T(8,128)S(1)} copy-done((s32[16,32]{1,0:T(8,128)S(1)}, s32[16,32]{1,0:T(8,128)}, u32[]{:S(2)}) %copy-start) | copy-done | bytes 2072
  2.0 0.0 copy-start.1
  2.0 0.7 %copy-done.1 = s32[16,32]{1,0:T(8,128)S(1)} copy-done((s32[16,32]{1,0:T(8,128)S(1)}, s32[16,32]{1,0:T(8,128)}, u32[]{:S(2)}) %copy-start.1) | copy-done | bytes 2072
  2.7 0.0 copy-start.2
  2.7 0.7 %copy-done.2 = s32[128]{0:T(128)S(1)} copy-done((s32[128]{0:T(128)S(1)}, s32[128]{0:T(128)}, u32[]{:S(2)}) %copy-start.2) | copy-done | bytes 536
  3.3 33.9 %fringe_fit.1 = (f32[16,16,32]{2,1,0:T(8,128)S(1)}, f32[16,2,64]{2,1,0:T(2,128)S(1)}, f32[2,16]{1,0:T(2,128)S(1)}) custom-call(bf16[4,4,1536,256]{3,2,1,0:T(8,128)(2,1)} %volts.1, s32[16,32]{1,0:T(8,128)S(1)} %copy-done, s32[16,32]{1,0:T(8,128)S(1)} %copy-done.1, s32[1,128]{1,0:T(1,128)S(1)} %bitcast.5, s32[1]{0:T(128)S(6)} %copy.8.ref), custom_call_target="tpu_custom_call" | custom-call | tf_op jit(solution)/shard_map/fringe_fit/pallas_call | solution.py:507
  37.2 0.7 %emit.1 = (f32[16,16,32]{2,1,0:T(8,128)}, f32[16,2,64]{2,1,0:T(2,128)}, f32[2,16]{1,0:T(2,128)}) custom-call(f32[16,16,32]{2,1,0:T(8,128)S(1)} %get-tuple-element.9.refs_0_, f32[16,2,64]{2,1,0:T(2,128)S(1)} %get-tuple-element.10.refs_1_, f32[2,16]{1,0:T(2,128)S(1)} %get-tuple-element.11.refs_2_), custom_call_target="tpu_custom_call" | custom-call | tf_op jit(solution)/shard_map/emit/pallas_call | solution.py:542
Async XLA Ops:
  1.3 0.7 %copy-start = (s32[16,32]{1,0:T(8,128)S(1)}, s32[16,32]{1,0:T(8,128)}, u32[]{:S(2)}) copy-start(s32[16,32]{1,0:T(8,128)} %dpk.1) | copy-start | bytes 6148
  2.0 0.7 %copy-start.1 = (s32[16,32]{1,0:T(8,128)S(1)}, s32[16,32]{1,0:T(8,128)}, u32[]{:S(2)}) copy-start(s32[16,32]{1,0:T(8,128)} %rpk.1) | copy-start | bytes 6148
  2.7 0.7 %copy-start.2 = (s32[128]{0:T(128)S(1)}, s32[128]{0:T(128)}, u32[]{:S(2)}) copy-start(s32[128]{0:T(128)} %param.8) | copy-start | bytes 1540

commit v3 on v2

--- a/solution.py
+++ b/solution.py
@@ -175,14 +175,13 @@
 
 
 def fused(
-    nchan, volts, dpk, rpk, order_in, ref, fringe_out, normal_out, rhs_out,
-    xbuf, dbuf, rbuf, order, vis, rv, pkl, pka, pnat, sbuf, rb2, zs, rz, wz, nat, rx,
-    vsem, isem, bsend, brecv, s1, r1, s2, r2, s3, r3, s4, r4, s5, r5,
+    nchan, rows, cols, volts, packed, ref, fringe_out, normal_out, rhs_out,
+    xbuf, vis, rv, pkl, pka, pnat, sbuf, rb2, zs, rz, wz, nat, rx,
+    vsem, bsend, brecv, s1, r1, s2, r2, s3, r3, s4, r4, s5, r5,
 ):
     i, j = lax.axis_index("tm"), lax.axis_index("chan")
     periods, chans, samples, width = volts.shape
     inputs = width // 2
-    rows, cols = dpk.shape
     chans_total = chans * nchan
     core, cx, cy = i % 2, (i // 2) % 2, i // 4
     sibling = i + 1 - 2 * core
@@ -203,13 +202,6 @@
     @pl.loop(0, periods * chans)
     def _(n):
         load(n).start()
-
-    small = [
-        pltpu.make_async_copy(src, dst, isem.at[n])
-        for n, (src, dst) in enumerate([(dpk, dbuf), (rpk, rbuf), (order_in, order)])
-    ]
-    for copy in small:
-        copy.start()
 
     barrier = pltpu.get_barrier_semaphore()
     mates = [(r, d) for r in range(4) for d in range(nchan) if r or d]
@@ -220,13 +212,8 @@
     for r in range(4):
         pl.semaphore_signal(barrier, inc=1, device_id=(chip(r, 1 - core), j), device_id_type=MESH)
 
-    for copy in small:
-        copy.wait()
     half = rows // 2
-    for h in range(2):
-        at = slice(h * half, h * half + half)
-        pkl[:, 2 * h * cols : (2 * h + 1) * cols] = dbuf[at, :]
-        pkl[:, (2 * h + 1) * cols : (2 * h + 2) * cols] = rbuf[at, :]
+    pkl[...] = packed[0:half, :]
     home = cy * 2 + cx
     pka[home, j] = pkl[...]
 
@@ -254,7 +241,7 @@
 
     hot = (
         lax.broadcasted_iota(jnp.int32, (inputs, inputs), 0)
-        == jnp.broadcast_to(order[...], (inputs, inputs))
+        == jnp.broadcast_to(packed[half : half + 1, :], (inputs, inputs))
     ).astype(jnp.float32)
     hot_t = hot.T
 
@@ -367,22 +354,27 @@
             out.append(acc[w] if wd == WD // 2 else cmul(acc[w], shifts[wd]))
         return [o[0] for o in out] + [o[1] for o in out]
 
-    @pl.loop(0, 4)
+    def plane(h, r):
+        return remote(
+            sbuf.at[h, r], rb2.at[h, r - 1], s2.at[h, r - 1], r2.at[h, r - 1], chip(r, core), j
+        )
+
+    @pl.loop(0, 8)
     def _(u):
-        r = 3 - u
-        for h in range(rows // 8):
-            values = window(chip(r, core) // 2, h)
-            for v, value in enumerate(values):
-                sbuf[r, v, h * 8 : h * 8 + 8, :] = value
+        h, r = u // 4, 3 - u % 4
+        for v, value in enumerate(window(chip(r, core) // 2, h)):
+            sbuf[h, r, v] = value
 
         @pl.when(r > 0)
         def _():
-            remote(sbuf.at[r], rb2.at[r - 1], s2.at[r - 1], r2.at[r - 1], chip(r, core), j).start()
+            plane(h, r).start()
 
     bins = WR * WD
-    row = lax.broadcasted_iota(jnp.int32, (bins * rows, inputs), 0)
-    col = lax.broadcasted_iota(jnp.int32, (bins * rows, inputs), 1)
-    w_row, kind = row // rows, col // rows
+    tall = 2 * bins * rows
+    row = lax.broadcasted_iota(jnp.int32, (tall, inputs), 0)
+    col = lax.broadcasted_iota(jnp.int32, (tall, inputs), 1)
+    p_row = row // (2 * bins * half) * half + row % half
+    w_row, kind = row // half % bins, col // rows
     ud = (2 * (w_row % WD) + 1 - WD).astype(jnp.float32) / WD
     ur = (2 * (w_row // WD) + 1 - WR).astype(jnp.float32) / WR
     coef = jnp.where(kind == 0, ud * ud, 0.0)
@@ -390,45 +382,49 @@
     coef = jnp.where(kind == 2, ur * ur, coef)
     coef = jnp.where(kind == 3, ud, coef)
     coef = jnp.where(kind == 4, ur, coef)
-    coef = jnp.where(row % rows == col % rows, coef, 0.0) * (1.0 / bins)
-
-    for r in (1, 2, 3):
-        remote(sbuf.at[r], rb2.at[r - 1], s2.at[r - 1], r2.at[r - 1], chip(r, core), j).wait()
-    total = (sbuf[0] + rb2[0]) + (rb2[1] + rb2[2])
-    shape3 = (2 * bins, rows, inputs)
-    auto = lax.broadcasted_iota(jnp.int32, shape3, 2) == (
-        lax.broadcasted_iota(jnp.int32, shape3, 1) + i * rows
-    )
-    total = jnp.where(auto, 0.0, total * scale).reshape(2 * bins * rows, inputs)
-    zs[...] = lax.dot_general(
-        hot_t, total, (((1,), (1,)), ((), ())),
-        precision=lax.Precision.HIGHEST, preferred_element_type=jnp.float32,
-    )
+    coef = jnp.where(p_row == col % rows, coef, 0.0) * (1.0 / bins)
 
     def group(g):
         return pl.ds(pl.multiple_of(g * cols, cols), cols)
 
-    copies = []
-    for d in range(1, nchan):
-        to = (j + d) % nchan
-        copies.append(remote(zs.at[group(to)], rz.at[d - 1], s3.at[d - 1], r3.at[d - 1], i, to))
-        copies[-1].start()
-    mine = zs[group(j), :]
-    for d, copy in enumerate(copies):
-        copy.wait()
-        mine = mine + rz[d]
-    fre, fim = mine[:, : bins * rows], mine[:, bins * rows :]
-    power = fre * fre + fim * fim
+    shape3 = (2 * bins, half, inputs)
+    lane3 = lax.broadcasted_iota(jnp.int32, shape3, 2)
+    row3 = lax.broadcasted_iota(jnp.int32, shape3, 1) + i * rows
+    zcopies = []
+    for h in range(2):
+        for r in (3, 2, 1):
+            plane(h, r).wait()
+        total = (sbuf[h, 0] + rb2[h, 0]) + (rb2[h, 1] + rb2[h, 2])
+        total = jnp.where(lane3 == row3 + h * half, 0.0, total * scale)
+        zs[h] = lax.dot_general(
+            hot_t, total.reshape(2 * bins * half, inputs), (((1,), (1,)), ((), ())),
+            precision=lax.Precision.HIGHEST, preferred_element_type=jnp.float32,
+        )
+        for d in range(1, nchan):
+            to = (j + d) % nchan
+            zcopies.append(
+                remote(zs.at[h, group(to)], rz.at[h, d - 1], s3.at[h, d - 1], r3.at[h, d - 1], i, to)
+            )
+            zcopies[-1].start()
+    parts = []
+    for h in range(2):
+        mine = zs[h, group(j), :]
+        for d in range(1, nchan):
+            zcopies[h * (nchan - 1) + d - 1].wait()
+            mine = mine + rz[h, d - 1]
+        parts.append(mine)
+    mine = jnp.concatenate(parts, axis=1)
     wz[group(j), :] = jnp.dot(
-        power, coef, precision=lax.Precision.HIGHEST, preferred_element_type=jnp.float32
+        mine * mine, coef, precision=lax.Precision.HIGHEST, preferred_element_type=jnp.float32
     )
     copies = []
     for d in range(1, nchan):
         to = (j + d) % nchan
         copies.append(remote(wz.at[group(j)], wz.at[group(j)], s4.at[d - 1], r4.at[d - 1], i, to))
         copies[-1].start()
-    turned = mine.T.reshape(2 * bins, rows, cols)
-    fringe_out[...] = jnp.swapaxes(turned, 0, 1)
+    for h in range(2):
+        turned = parts[h].T.reshape(2 * bins, half, cols)
+        fringe_out[h * half : (h + 1) * half] = jnp.swapaxes(turned, 0, 1)
     for copy in copies:
         copy.wait()
     natural = jnp.dot(
@@ -503,34 +499,33 @@
         jax.ShapeDtypeStruct((rows, 2, 2 * inputs // nchan), f32),
         jax.ShapeDtypeStruct((2, rows), f32),
     )
-    hbm = pl.BlockSpec(memory_space=pltpu.HBM)
+    half = rows // 2
+    packed = jnp.concatenate([delay_peak[:half], rate_peak[:half], delay_peak[half:], rate_peak[half:]], 1)
+    packed = jnp.concatenate([packed, jnp.broadcast_to(station_order, (half, inputs))], 0)
     results = pl.pallas_call(
-        functools.partial(fused, nchan),
+        functools.partial(fused, nchan, rows, cols),
         out_shape=out_shape,
-        in_specs=[hbm, hbm, hbm, hbm, pl.BlockSpec(memory_space=pltpu.SMEM)],
+        in_specs=[pl.BlockSpec(memory_space=pl.ANY), vmem, pl.BlockSpec(memory_space=pltpu.SMEM)],
         out_specs=(vmem, vmem, vmem),
         scratch_shapes=[
             pltpu.VMEM((steps, samples, width), volts.dtype),
-            pltpu.VMEM((rows, cols), jnp.int32),
-            pltpu.VMEM((rows, cols), jnp.int32),
-            pltpu.VMEM((1, inputs), jnp.int32),
             pltpu.VMEM((2, steps, 2, 4 * rows, inputs), f32),
             pltpu.VMEM((steps, 2, 4 * rows, inputs), f32),
             pltpu.VMEM((rows // 2, 4 * cols), jnp.int32),
             pltpu.VMEM((4, nchan, rows // 2, 4 * cols), jnp.int32),
             pltpu.VMEM((2, 4 * rows, inputs), jnp.int32),
-            pltpu.VMEM((4, 2 * bins, rows, inputs), f32),
-            pltpu.VMEM((3, 2 * bins, rows, inputs), f32),
-            pltpu.VMEM((inputs, 2 * bins * rows), f32),
-            pltpu.VMEM((nchan - 1, cols, 2 * bins * rows), f32),
+            pltpu.VMEM((2, 4, 2 * bins, half, inputs), f32),
+            pltpu.VMEM((2, 3, 2 * bins, half, inputs), f32),
+            pltpu.VMEM((2, inputs, 2 * bins * half), f32),
+            pltpu.VMEM((2, nchan - 1, cols, 2 * bins * half), f32),
             pltpu.VMEM((inputs, inputs), f32),
             pltpu.VMEM((inputs, inputs), f32),
             pltpu.VMEM((TM, rows, inputs), f32),
-            dma((steps,)), dma((3,)),
+            dma((steps,)),
             dma((4 * nchan - 1,)), dma((4 * nchan - 1,)),
             dma((steps,)), dma((steps,)),
-            dma((3,)), dma((3,)),
-            dma((nchan - 1,)), dma((nchan - 1,)),
+            dma((2, 3)), dma((2, 3)),
+            dma((2, nchan - 1)), dma((2, nchan - 1)),
             dma((nchan - 1,)), dma((nchan - 1,)),
             dma((TM - 1,)), dma((TM - 1,)),
         ],
@@ -538,7 +533,7 @@
             collective_id=0, has_side_effects=True, vmem_limit_bytes=48 * 1024 * 1024
         ),
         name="fringe_fit",
-    )(volts, delay_peak, rate_peak, station_order.reshape(1, inputs), ref_station)
+    )(volts, packed, ref_station)
     fringe, normal, rhs = pl.pallas_call(
         emit, out_shape=out_shape, in_specs=[vmem] * 3, out_specs=(vmem,) * 3, name="emit",
         compiler_params=pltpu.CompilerParams(vmem_limit_bytes=4 * 1024 * 1024),

time: 38.2 us -> 36.7 us (0.961)
  Pallas kernels: 34.6 us -> 33.7 us
  local copies, waits for them, and re-layouts: 2.04 us -> 1.4 us
    unnamed x6 -> x0, local copies, waits for them, and re-layouts: 2.04 us -> none
    pallas_call x1, Pallas kernels: 33.9 us -> 33 us  [fused_body(): pl.pallas_call(functools.partial(fused, nchan, rows, cols), out_shape=out...]
    slice x0 -> x1, local copies, waits for them, and re-layouts: none -> 0.74 us  [fused_body(): delay_peak[:half]]
    broadcast_in_dim x0 -> x1, local copies, waits for them, and re-layouts: none -> 0.66 us  [fused_body(): jnp.broadcast_to(station_order, (half, inputs))]
where the time goes in v3:
time: 36.7 us; the launch traced here: 36.5 us
  Pallas kernels  33.7 us (92%)
  local copies, waits for them, and re-layouts  1.4 us (4%)
  between operations  1.29 us (4%)
    pallas_call x1, Pallas kernels, fused_body(): pl.pallas_call(functools.partial(fused, nchan, rows, cols), out_shape=out...  33 us
    slice x1, local copies, waits for them, and re-layouts, fused_body(): delay_peak[:half]  0.74 us

profile of v3, /device:TPU:0, one launch (start us, length us, event | category | flops | bytes accessed | tf_op | source)
XLA Modules:
  0.0 36.5 jit_solution(17535720831481636528)
XLA Ops:
  1.3 0.7 %broadcast_in_dim.3 = s32[8,128]{1,0:T(8,128)S(1)} broadcast(s32[128]{0:T(128)} %param.8), dimensions={1} | broadcast | bytes 4608 | tf_op jit(solution)/shard_map/broadcast_in_dim | solution.py:504
  1.9 0.7 %fusion = (s32[8,32]{1,0:T(8,128)S(1)}, s32[8,32]{1,0:T(8,128)S(1)}, s32[8,32]{1,0:T(8,128)S(1)}, s32[8,32]{1,0:T(8,128)S(1)}) fusion(s32[16,32]{1,0:T(8,128)} %param.6, s32[16,32]{1,0:T(8,128)} %param.7), kind=kLoop, calls=%fused_computation.1 | loop fusion | bytes 8192 | tf_op jit(solution)/shard_map/slice | solution.py:503
  2.7 0.1 pad_add_fusion.packed
  2.8 33.0 %fringe_fit.1 = (f32[16,16,32]{2,1,0:T(8,128)S(1)}, f32[16,2,64]{2,1,0:T(2,128)S(1)}, f32[2,16]{1,0:T(2,128)S(1)}) custom-call(bf16[4,4,1536,256]{3,2,1,0:T(8,128)(2,1)} %volts.1, s32[16,128]{1,0:T(8,128)S(1)} %pad_add_fusion.packed, s32[1]{0:T(128)S(6)} %copy.8.ref), custom_call_target="tpu_custom_call" | custom-call | tf_op jit(solution)/shard_map/fringe_fit/pallas_call | solution.py:505
  35.8 0.7 %emit.1 = (f32[16,16,32]{2,1,0:T(8,128)}, f32[16,2,64]{2,1,0:T(2,128)}, f32[2,16]{1,0:T(2,128)}) custom-call(f32[16,16,32]{2,1,0:T(8,128)S(1)} %get-tuple-element.9.refs_0_, f32[16,2,64]{2,1,0:T(2,128)S(1)} %get-tuple-element.10.refs_1_, f32[2,16]{1,0:T(2,128)S(1)} %get-tuple-element.11.refs_2_), custom_call_target="tpu_custom_call" | custom-call | tf_op jit(solution)/shard_map/emit/pallas_call | solution.py:537
